TPU v7x, 512 devices: a whole 4x8x8 slice. The times are simulated.
512 devices in a mesh: blk: 128 (over y, z, core), pitch: 4 (over x).
Axes of the slice: x: 4, y: 8, z: 8, core: 2. Of those that a mesh axis runs over, the one named last changes fastest.
Arguments:
- states: float32 [2, 5, 1024, 32, 128], P(None, None, 'blk', 'pitch'), may hold values from -6 to 6
- time_steps: float32 [2, 1024, 32, 128], P(None, 'blk', 'pitch'), may hold values from 0.05 to 0.4
- speeds: float32 [2, 5, 3], replicated, may hold values from 0.2 to 0.7
- band_src: int32 [2, 1024, 3], P(None, 'blk'), may hold values from 0 to 1023, as said below
- band_frac: int32 [2, 1024, 3], P(None, 'blk'), may hold values from 0 to 65536, as said below
Outputs:
- states_out: float32 [2, 5, 1024, 32, 128], P(None, None, 'blk', 'pitch')
- arrivals: float32 [2, 1024, 480], P(None, 'blk', 'pitch')
Inputs may be any that keep to these rules, and one draw needn't show every extreme that they name: `band_src`: row j of either table names, in its 3 slots in some order, rows j - 1, j, j + 1 of the other blade row where they exist and j itself otherwise; every named row lies within one row of j. `band_frac`: A slot naming a row that does not intersect the receiving row has fraction 0; a row's fractions sum to at most 65536.
All inputs are finite; a program needn't handle non-finite values.
Results may differ from a plain program's by a relative error of at most 0.000075.
Values sent between devices are 32-bit elements; how exact they have to be, the bound alone decides.
A program may use at most 64 MiB of HBM per device.

v0:
```python
import math

import jax
import jax.numpy as jnp
from jax import lax
from jax.sharding import PartitionSpec as P

NH = 48


viscosity = 0.15
section_weights = (1.0 / 3.0, 0.5, 1.0)


def padded(block, sides, width, periodic):
    for axis, dim in sides:
        count = lax.axis_size(axis)
        forward = [(i, i + 1) for i in range(count - 1)]
        if periodic:
            forward.append((count - 1, 0))
        backward = [(target, source) for source, target in forward]
        low = lax.ppermute(
            lax.slice_in_dim(block, block.shape[dim] - width, None, axis=dim), axis, forward
        )
        high = lax.ppermute(lax.slice_in_dim(block, 0, width, axis=dim), axis, backward)
        block = jnp.concatenate([low, block, high], axis=dim)
    return block


def harmonic_table(places, period, count):
    orders = jnp.arange(count, dtype=jnp.int32)
    cos_phase = (places[:, None] * orders[None, :] % period).astype(jnp.float32)
    sin_phase = (places[:, None] * (orders[None, :] + 1) % period).astype(jnp.float32)
    factor = jnp.where(orders == 0, 1.0, 2.0).astype(jnp.float32) / period
    cos_cols = jnp.cos(2.0 * math.pi * cos_phase / period) * factor[None, :]
    sin_cols = jnp.sin(2.0 * math.pi * sin_phase / period) * (2.0 / period)
    return jnp.concatenate([cos_cols, sin_cols], 1)


def residual(extended, speeds):
    centre = extended[:, :, 1:-1, 1:-1, :]
    zero_face = jnp.zeros_like(centre[..., :1])
    axial_low = jnp.concatenate([zero_face, centre[..., :-1]], 4)
    axial_high = jnp.concatenate([centre[..., 1:], zero_face], 4)
    radial_low = extended[:, :, :-2, 1:-1, :]
    radial_high = extended[:, :, 2:, 1:-1, :]
    pitch_low = extended[:, :, 1:-1, :-2, :]
    pitch_high = extended[:, :, 1:-1, 2:, :]
    speed_axial = speeds[:, :, 0][:, :, None, None, None]
    speed_radial = speeds[:, :, 1][:, :, None, None, None]
    speed_pitch = speeds[:, :, 2][:, :, None, None, None]
    neighbours = axial_low + axial_high + radial_low + radial_high + pitch_low + pitch_high
    return (
        -speed_axial * (centre - axial_low)
        - speed_radial * (centre - radial_low)
        - speed_pitch * (centre - pitch_low)
        + viscosity * (neighbours - 6.0 * centre)
    )


def pick_rows(source_table, indices):
    return source_table[indices]


def shards(states, time_steps, speeds, band_src, band_frac):
    var_count = states.shape[1]
    rows_here = states.shape[2]
    pitch_here = states.shape[3]
    block_index = lax.axis_index("blk")
    field = states
    for weight_of in section_weights:
        pitched = padded(field, (("pitch", 3),), 1, True)
        extended = padded(pitched, (("blk", 2),), 1, False)
        field = states + weight_of * time_steps[:, None] * residual(extended, speeds)
    planes = jnp.stack([field[0, :, :, :, -1], field[1, :, :, :, 0]])
    period = pitch_here * lax.axis_size("pitch")
    places = lax.axis_index("pitch") * pitch_here + jnp.arange(pitch_here, dtype=jnp.int32)
    table = harmonic_table(places, period, NH)
    partial_coef = jnp.einsum("wvrp,pm->wrvm", planes, table, precision=lax.Precision.HIGHEST)
    partial_coef = partial_coef.reshape(2, rows_here, var_count * 2 * NH)
    coef_cols = lax.psum_scatter(partial_coef, "pitch", scatter_dimension=2, tiled=True)
    source_rows = padded(coef_cols, (("blk", 1),), 1, False)
    local_index = band_src - (block_index * rows_here - 1)
    picked = jax.vmap(pick_rows)(source_rows[::-1], local_index)
    weights = band_frac.astype(jnp.float32) * (1.0 / 65536.0)
    arrivals = jnp.sum(weights[..., None] * picked, axis=2)
    return (field, arrivals)


def solution(mesh):
    return jax.shard_map(
        shards,
        mesh=mesh,
        in_specs=(
            P(None, None, "blk", "pitch", None),
            P(None, "blk", "pitch", None),
            P(),
            P(None, "blk", None),
            P(None, "blk", None),
        ),
        out_specs=(P(None, None, "blk", "pitch", None), P(None, "blk", "pitch")),
        check_vma=False,
    )
```

profile of v0, /device:TPU:32, one launch (start us, length us, event | category | flops | bytes accessed | tf_op | source)
XLA Modules:
  0.0 98.2 jit_solution(18079608087794586349)
XLA Ops:
  0.6 1.1 %fusion.62 = (f32[2,5,8,1,128]{4,3,2,1,0:T(1,128)S(1)}, f32[2,5,8,1,128]{4,3,2,1,0:T(1,128)S(1)}) fusion(f32[2,5,8,8,128]{4,3,2,1,0:T(8,128)} %param.5), kind=kLoop, calls=%fused_computation.123 | loop fusion | bytes 163840 | tf_op jit(solution)/shard_map/slice | solution.py:23
  1.8 3.4 %collective-permute-start = (f32[2,5,8,1,128]{4,2,3,1,0:T(8,128)S(1)}, f32[2,5,8,1,128]{4,2,3,1,0:T(8,128)S(1)}, u32[]{:S(2)}, u32[]{:S(2)}) collective-permute-start(f32[2,5,8,1,128]{4,2,3,1,0:T(8,128)S(1)} %bitcast.65), channel_id=1, source_target_pairs={{0,1},{1,2},{2,3},{3,0},{4,5},{5,6},{6,7},{7,4},{8,9},{9,10},{10,1... | collective-permute-start | bytes 122888 | tf_op jit(solution)/shard_map/ppermute | solution.py:22
  5.2 0.0 copy-start.2
  5.2 3.8 %collective-permute-start.1 = (f32[2,5,8,1,128]{4,2,3,1,0:T(8,128)S(1)}, f32[2,5,8,1,128]{4,2,3,1,0:T(8,128)S(1)}, u32[]{:S(2)}, u32[]{:S(2)}) collective-permute-start(f32[2,5,8,1,128]{4,2,3,1,0:T(8,128)S(1)} %bitcast.63), channel_id=1, source_target_pairs={{1,0},{2,1},{3,2},{0,3},{5,4},{6,5},{7,6},{4,7},{9,8},{10,9},{11,1... | collective-permute-start | bytes 122888 | tf_op jit(solution)/shard_map/ppermute | solution.py:25
  9.0 0.0 copy-start
  9.0 1.3 %fusion.61 = (f32[2,5,8,8,127]{4,3,2,1,0:T(8,128)S(1)}, f32[2,5,8,8,127]{4,3,2,1,0:T(8,128)S(1)}) fusion(f32[2,5,8,8,128]{4,3,2,1,0:T(8,128)} %param.5), kind=kLoop, calls=%fused_computation.122 | loop fusion | bytes 1300480 | tf_op jit(solution)/shard_map/slice | solution.py:43
  10.3 0.0 copy-done.2
  10.3 0.1 fusion.40
  10.5 0.0 collective-permute-done
  10.5 0.7 collective-permute-done.1
  11.2 0.0 copy-done
  11.3 1.9 %collective-permute-start.2 = (f32[2,5,1,10,128]{4,0,3,2,1:T(2,128)S(1)}, f32[2,5,1,10,128]{4,0,3,2,1:T(2,128)S(1)}, u32[]{:S(2)}, u32[]{:S(2)}) collective-permute-start(f32[2,5,1,10,128]{4,0,3,2,1:T(2,128)S(1)} %copy.336), channel_id=1, source_target_pairs={{0,4},{4,8},{8,12},{12,16},{16,20},{20,24},{24,28},{28,32},{32,36}... | collective-permute-start | bytes 153608 | tf_op jit(solution)/shard_map/ppermute | solution.py:22
  13.2 0.0 copy-start.3
  13.3 9.0 %collective-permute-start.3 = (f32[2,5,1,10,128]{4,0,3,2,1:T(2,128)S(1)}, f32[2,5,1,10,128]{4,0,3,2,1:T(2,128)S(1)}, u32[]{:S(2)}, u32[]{:S(2)}) collective-permute-start(f32[2,5,1,10,128]{4,0,3,2,1:T(2,128)S(1)} %copy.339), channel_id=1, source_target_pairs={{4,0},{8,4},{12,8},{16,12},{20,16},{24,20},{28,24},{32,28},{36,32}... | collective-permute-start | bytes 153608 | tf_op jit(solution)/shard_map/ppermute | solution.py:25
  22.3 0.0 copy-done.3
  22.3 0.0 collective-permute-done.2
  22.3 1.7 %collective-permute-done.3 = f32[2,5,1,10,128]{4,0,3,2,1:T(2,128)S(1)} collective-permute-done((f32[2,5,1,10,128]{4,0,3,2,1:T(2,128)S(1)}, f32[2,5,1,10,128]{4,0,3,2,1:T(2,128)S(1)}, u32[]{:S(2)}, u32[]{:S(2)}) %collective-permute-start.3) | collective-permute-done | bytes 51232 | tf_op jit(solution)/shard_map/ppermute | solution.py:25
  24.0 0.5 fusion.27
  24.5 0.1 fusion.60
  24.6 0.0 copy-start.4
  24.6 4.7 %collective-permute-start.5 = (f32[2,5,8,1,128]{4,2,3,1,0:T(8,128)S(1)}, f32[2,5,8,1,128]{4,2,3,1,0:T(8,128)S(1)}, u32[]{:S(2)}, u32[]{:S(2)}) collective-permute-start(f32[2,5,8,1,128]{4,2,3,1,0:T(8,128)S(1)} %bitcast.67), channel_id=1, source_target_pairs={{1,0},{2,1},{3,2},{0,3},{5,4},{6,5},{7,6},{4,7},{9,8},{10,9},{11,1... | collective-permute-start | bytes 122888 | tf_op jit(solution)/shard_map/ppermute | solution.py:25
  29.3 1.9 %collective-permute-start.4 = (f32[2,5,8,1,128]{4,2,3,1,0:T(8,128)S(1)}, f32[2,5,8,1,128]{4,2,3,1,0:T(8,128)S(1)}, u32[]{:S(2)}, u32[]{:S(2)}) collective-permute-start(f32[2,5,8,1,128]{4,2,3,1,0:T(8,128)S(1)} %bitcast.66), channel_id=1, source_target_pairs={{0,1},{1,2},{2,3},{3,0},{4,5},{5,6},{6,7},{7,4},{8,9},{9,10},{10,1... | collective-permute-start | bytes 122888 | tf_op jit(solution)/shard_map/ppermute | solution.py:22
  31.2 0.0 copy-done.4
  31.2 0.0 collective-permute-done.5
  31.3 5.1 %collective-permute-done.4 = f32[2,5,8,1,128]{4,2,3,1,0:T(8,128)S(1)} collective-permute-done((f32[2,5,8,1,128]{4,2,3,1,0:T(8,128)S(1)}, f32[2,5,8,1,128]{4,2,3,1,0:T(8,128)S(1)}, u32[]{:S(2)}, u32[]{:S(2)}) %collective-permute-start.4) | collective-permute-done | bytes 40992 | tf_op jit(solution)/shard_map/ppermute | solution.py:22
  36.5 1.9 %collective-permute-start.6 = (f32[2,5,1,10,128]{4,0,3,2,1:T(2,128)S(1)}, f32[2,5,1,10,128]{4,0,3,2,1:T(2,128)S(1)}, u32[]{:S(2)}, u32[]{:S(2)}) collective-permute-start(f32[2,5,1,10,128]{4,0,3,2,1:T(2,128)S(1)} %copy.346), channel_id=1, source_target_pairs={{0,4},{4,8},{8,12},{12,16},{16,20},{20,24},{24,28},{28,32},{32,36}... | collective-permute-start | bytes 153608 | tf_op jit(solution)/shard_map/ppermute | solution.py:22
  38.4 7.0 %collective-permute-start.7 = (f32[2,5,1,10,128]{4,0,3,2,1:T(2,128)S(1)}, f32[2,5,1,10,128]{4,0,3,2,1:T(2,128)S(1)}, u32[]{:S(2)}, u32[]{:S(2)}) collective-permute-start(f32[2,5,1,10,128]{4,0,3,2,1:T(2,128)S(1)} %copy.349), channel_id=1, source_target_pairs={{4,0},{8,4},{12,8},{16,12},{20,16},{24,20},{28,24},{32,28},{36,32}... | collective-permute-start | bytes 153608 | tf_op jit(solution)/shard_map/ppermute | solution.py:25
  45.4 0.2 fusion.59
  45.6 0.0 collective-permute-done.6
  45.6 1.6 %collective-permute-done.7 = f32[2,5,1,10,128]{4,0,3,2,1:T(2,128)S(1)} collective-permute-done((f32[2,5,1,10,128]{4,0,3,2,1:T(2,128)S(1)}, f32[2,5,1,10,128]{4,0,3,2,1:T(2,128)S(1)}, u32[]{:S(2)}, u32[]{:S(2)}) %collective-permute-start.7) | collective-permute-done | bytes 51232 | tf_op jit(solution)/shard_map/ppermute | solution.py:25
  47.2 0.5 fusion.16
  47.7 0.1 fusion.58
  47.7 0.0 copy-start.5
  47.7 1.9 %collective-permute-start.8 = (f32[2,5,8,1,128]{4,2,3,1,0:T(8,128)S(1)}, f32[2,5,8,1,128]{4,2,3,1,0:T(8,128)S(1)}, u32[]{:S(2)}, u32[]{:S(2)}) collective-permute-start(f32[2,5,8,1,128]{4,2,3,1,0:T(8,128)S(1)} %bitcast.64), channel_id=1, source_target_pairs={{0,1},{1,2},{2,3},{3,0},{4,5},{5,6},{6,7},{7,4},{8,9},{9,10},{10,1... | collective-permute-start | bytes 122888 | tf_op jit(solution)/shard_map/ppermute | solution.py:22
  49.7 5.1 %collective-permute-start.9 = (f32[2,5,8,1,128]{4,2,3,1,0:T(8,128)S(1)}, f32[2,5,8,1,128]{4,2,3,1,0:T(8,128)S(1)}, u32[]{:S(2)}, u32[]{:S(2)}) collective-permute-start(f32[2,5,8,1,128]{4,2,3,1,0:T(8,128)S(1)} %bitcast.62), channel_id=1, source_target_pairs={{1,0},{2,1},{3,2},{0,3},{5,4},{6,5},{7,6},{4,7},{9,8},{10,9},{11,1... | collective-permute-start | bytes 122888 | tf_op jit(solution)/shard_map/ppermute | solution.py:25
  54.8 0.0 copy-done.5
  54.8 0.1 copy.365
  54.9 0.1 reshape.39
  55.0 0.1 copy.362
  55.1 1.3 %dynamic-slice = u32[1]{0:T(128)} dynamic-slice(u32[512]{0:T(512)} %constant.100, u32[]{:T(128)S(6)} %add.145), dynamic_slice_sizes={1} | dynamic-slice | bytes 12
  57.0 0.0 collective-permute-done.8
  57.0 0.0 collective-permute-done.9
  57.1 1.9 %collective-permute-start.10 = (f32[2,5,1,10,128]{4,0,3,2,1:T(2,128)S(1)}, f32[2,5,1,10,128]{4,0,3,2,1:T(2,128)S(1)}, u32[]{:S(2)}, u32[]{:S(2)}) collective-permute-start(f32[2,5,1,10,128]{4,0,3,2,1:T(2,128)S(1)} %copy.356), channel_id=1, source_target_pairs={{0,4},{4,8},{8,12},{12,16},{16,20},{20,24},{24,28},{28,32},{32,36}... | collective-permute-start | bytes 153608 | tf_op jit(solution)/shard_map/ppermute | solution.py:22
  59.1 7.0 %collective-permute-start.11 = (f32[2,5,1,10,128]{4,0,3,2,1:T(2,128)S(1)}, f32[2,5,1,10,128]{4,0,3,2,1:T(2,128)S(1)}, u32[]{:S(2)}, u32[]{:S(2)}) collective-permute-start(f32[2,5,1,10,128]{4,0,3,2,1:T(2,128)S(1)} %copy.359), channel_id=1, source_target_pairs={{4,0},{8,4},{12,8},{16,12},{20,16},{24,20},{28,24},{32,28},{36,32}... | collective-permute-start | bytes 153608 | tf_op jit(solution)/shard_map/ppermute | solution.py:25
  66.0 0.2 fusion.57
  66.2 0.0 collective-permute-done.10
  66.2 1.6 %collective-permute-done.11 = f32[2,5,1,10,128]{4,0,3,2,1:T(2,128)S(1)} collective-permute-done((f32[2,5,1,10,128]{4,0,3,2,1:T(2,128)S(1)}, f32[2,5,1,10,128]{4,0,3,2,1:T(2,128)S(1)}, u32[]{:S(2)}, u32[]{:S(2)}) %collective-permute-start.11) | collective-permute-done | bytes 51232 | tf_op jit(solution)/shard_map/ppermute | solution.py:25
  67.8 0.5 fusion.5
  68.3 0.0 copy-start.1
  68.3 0.3 slice_reduce_fusion.1
  68.6 0.2 convolution_bitcast_fusion
  68.8 0.1 reshape.51
  68.9 0.1 copy-done.1
  69.0 17.2 %all-reduce.6 = f32[2,8,480]{2,0,1:T(2,128)S(1)} all-reduce(f32[2,8,480]{2,0,1:T(2,128)S(1)} %reshape.51), channel_id=2, replica_groups=mesh['blk'=128,'pitch'=4] {'pitch'}, use_global_device_ids=true, to_apply=%region_0.1.clone | all-reduce | flops 7680 | bytes 61440
  86.3 0.1 constant_dynamic-slice_fusion.1
  86.4 1.9 %collective-permute-start.12 = (f32[2,1,120]{2,0,1:T(2,128)S(1)}, f32[2,1,120]{2,0,1:T(2,128)S(1)}, u32[]{:S(2)}, u32[]{:S(2)}) collective-permute-start(f32[2,1,120]{2,0,1:T(2,128)S(1)} %get-tuple-element.32), channel_id=1, source_target_pairs={{0,4},{4,8},{8,12},{12,16},{16,20},{20,24},{24,28},{28,32},{32,36}... | collective-permute-start | bytes 2888 | tf_op jit(solution)/shard_map/ppermute | solution.py:22
  88.3 7.0 %collective-permute-start.13 = (f32[2,1,120]{2,0,1:T(2,128)S(1)}, f32[2,1,120]{2,0,1:T(2,128)S(1)}, u32[]{:S(2)}, u32[]{:S(2)}) collective-permute-start(f32[2,1,120]{2,0,1:T(2,128)S(1)} %get-tuple-element.33), channel_id=1, source_target_pairs={{4,0},{8,4},{12,8},{16,12},{20,16},{24,20},{28,24},{32,28},{36,32}... | collective-permute-start | bytes 2888 | tf_op jit(solution)/shard_map/ppermute | solution.py:25
  95.3 0.1 constant_dynamic-slice_fusion.2
  95.3 0.0 collective-permute-done.12
  95.3 1.2 %collective-permute-done.13 = f32[2,1,120]{2,0,1:T(2,128)S(1)} collective-permute-done((f32[2,1,120]{2,0,1:T(2,128)S(1)}, f32[2,1,120]{2,0,1:T(2,128)S(1)}, u32[]{:S(2)}, u32[]{:S(2)}) %collective-permute-start.13) | collective-permute-done | bytes 992 | tf_op jit(solution)/shard_map/ppermute | solution.py:25
  96.6 0.9 gather_fusion
  97.5 0.7 multiply_reduce_fusion
  (26 shorter events, 0.4 us)
Async XLA Ops:
  1.8 8.7 %collective-permute-start = (f32[2,5,8,1,128]{4,2,3,1,0:T(8,128)S(1)}, f32[2,5,8,1,128]{4,2,3,1,0:T(8,128)S(1)}, u32[]{:S(2)}, u32[]{:S(2)}) collective-permute-start(f32[2,5,8,1,128]{4,2,3,1,0:T(8,128)S(1)} %bitcast.65), channel_id=1, source_target_pairs={{0,1},{1,2},{2,3},{3,0},{4,5},{5,6},{6,7},{7,4},{8,9},{9,10},{10,1... | collective-permute-start | bytes 122888 | tf_op jit(solution)/shard_map/ppermute | solution.py:22
  5.2 5.1 %copy-start.2 = (f32[2,8,8,128]{3,2,1,0:T(8,128)S(1)}, f32[2,8,8,128]{3,2,1,0:T(8,128)}, u32[]{:S(2)}) copy-start(f32[2,8,8,128]{3,2,1,0:T(8,128)} %param.6) | copy-start | bytes 196612
  5.2 6.0 %collective-permute-start.1 = (f32[2,5,8,1,128]{4,2,3,1,0:T(8,128)S(1)}, f32[2,5,8,1,128]{4,2,3,1,0:T(8,128)S(1)}, u32[]{:S(2)}, u32[]{:S(2)}) collective-permute-start(f32[2,5,8,1,128]{4,2,3,1,0:T(8,128)S(1)} %bitcast.63), channel_id=1, source_target_pairs={{1,0},{2,1},{3,2},{0,3},{5,4},{6,5},{7,6},{4,7},{9,8},{10,9},{11,1... | collective-permute-start | bytes 122888 | tf_op jit(solution)/shard_map/ppermute | solution.py:25
  9.0 2.2 %copy-start = (f32[2,5,8,8,128]{4,3,2,1,0:T(8,128)S(1)}, f32[2,5,8,8,128]{4,3,2,1,0:T(8,128)}, u32[]{:S(2)}) copy-start(f32[2,5,8,8,128]{4,3,2,1,0:T(8,128)} %param.5) | copy-start | bytes 983044
  11.3 11.0 %collective-permute-start.2 = (f32[2,5,1,10,128]{4,0,3,2,1:T(2,128)S(1)}, f32[2,5,1,10,128]{4,0,3,2,1:T(2,128)S(1)}, u32[]{:S(2)}, u32[]{:S(2)}) collective-permute-start(f32[2,5,1,10,128]{4,0,3,2,1:T(2,128)S(1)} %copy.336), channel_id=1, source_target_pairs={{0,4},{4,8},{8,12},{12,16},{16,20},{20,24},{24,28},{28,32},{32,36}... | collective-permute-start | bytes 153608 | tf_op jit(solution)/shard_map/ppermute | solution.py:22
  13.2 9.1 %copy-start.3 = (f32[2,5,3]{1,0,2:T(2,128)S(1)}, f32[2,5,3]{1,0,2:T(2,128)}, u32[]{:S(2)}) copy-start(f32[2,5,3]{1,0,2:T(2,128)} %param.7) | copy-start | bytes 364
  13.3 10.8 %collective-permute-start.3 = (f32[2,5,1,10,128]{4,0,3,2,1:T(2,128)S(1)}, f32[2,5,1,10,128]{4,0,3,2,1:T(2,128)S(1)}, u32[]{:S(2)}, u32[]{:S(2)}) collective-permute-start(f32[2,5,1,10,128]{4,0,3,2,1:T(2,128)S(1)} %copy.339), channel_id=1, source_target_pairs={{4,0},{8,4},{12,8},{16,12},{20,16},{24,20},{28,24},{32,28},{36,32}... | collective-permute-start | bytes 153608 | tf_op jit(solution)/shard_map/ppermute | solution.py:25
  24.6 6.7 %copy-start.4 = (s32[2,8,3]{1,0,2:T(2,128)S(1)}, s32[2,8,3]{1,0,2:T(2,128)}, u32[]{:S(2)}) copy-start(s32[2,8,3]{1,0,2:T(2,128)} %param.9) | copy-start | bytes 580
  24.6 6.7 %collective-permute-start.5 = (f32[2,5,8,1,128]{4,2,3,1,0:T(8,128)S(1)}, f32[2,5,8,1,128]{4,2,3,1,0:T(8,128)S(1)}, u32[]{:S(2)}, u32[]{:S(2)}) collective-permute-start(f32[2,5,8,1,128]{4,2,3,1,0:T(8,128)S(1)} %bitcast.67), channel_id=1, source_target_pairs={{1,0},{2,1},{3,2},{0,3},{5,4},{6,5},{7,6},{4,7},{9,8},{10,9},{11,1... | collective-permute-start | bytes 122888 | tf_op jit(solution)/shard_map/ppermute | solution.py:25
  29.3 7.1 %collective-permute-start.4 = (f32[2,5,8,1,128]{4,2,3,1,0:T(8,128)S(1)}, f32[2,5,8,1,128]{4,2,3,1,0:T(8,128)S(1)}, u32[]{:S(2)}, u32[]{:S(2)}) collective-permute-start(f32[2,5,8,1,128]{4,2,3,1,0:T(8,128)S(1)} %bitcast.66), channel_id=1, source_target_pairs={{0,1},{1,2},{2,3},{3,0},{4,5},{5,6},{6,7},{7,4},{8,9},{9,10},{10,1... | collective-permute-start | bytes 122888 | tf_op jit(solution)/shard_map/ppermute | solution.py:22
  36.5 9.1 %collective-permute-start.6 = (f32[2,5,1,10,128]{4,0,3,2,1:T(2,128)S(1)}, f32[2,5,1,10,128]{4,0,3,2,1:T(2,128)S(1)}, u32[]{:S(2)}, u32[]{:S(2)}) collective-permute-start(f32[2,5,1,10,128]{4,0,3,2,1:T(2,128)S(1)} %copy.346), channel_id=1, source_target_pairs={{0,4},{4,8},{8,12},{12,16},{16,20},{20,24},{24,28},{28,32},{32,36}... | collective-permute-start | bytes 153608 | tf_op jit(solution)/shard_map/ppermute | solution.py:22
  38.4 8.7 %collective-permute-start.7 = (f32[2,5,1,10,128]{4,0,3,2,1:T(2,128)S(1)}, f32[2,5,1,10,128]{4,0,3,2,1:T(2,128)S(1)}, u32[]{:S(2)}, u32[]{:S(2)}) collective-permute-start(f32[2,5,1,10,128]{4,0,3,2,1:T(2,128)S(1)} %copy.349), channel_id=1, source_target_pairs={{4,0},{8,4},{12,8},{16,12},{20,16},{24,20},{28,24},{32,28},{36,32}... | collective-permute-start | bytes 153608 | tf_op jit(solution)/shard_map/ppermute | solution.py:25
  47.7 7.1 %copy-start.5 = (s32[2,8,3]{1,0,2:T(2,128)S(1)}, s32[2,8,3]{1,0,2:T(2,128)}, u32[]{:S(2)}) copy-start(s32[2,8,3]{1,0,2:T(2,128)} %param.8) | copy-start | bytes 580
  47.7 9.3 %collective-permute-start.8 = (f32[2,5,8,1,128]{4,2,3,1,0:T(8,128)S(1)}, f32[2,5,8,1,128]{4,2,3,1,0:T(8,128)S(1)}, u32[]{:S(2)}, u32[]{:S(2)}) collective-permute-start(f32[2,5,8,1,128]{4,2,3,1,0:T(8,128)S(1)} %bitcast.64), channel_id=1, source_target_pairs={{0,1},{1,2},{2,3},{3,0},{4,5},{5,6},{6,7},{7,4},{8,9},{9,10},{10,1... | collective-permute-start | bytes 122888 | tf_op jit(solution)/shard_map/ppermute | solution.py:22
  49.7 7.4 %collective-permute-start.9 = (f32[2,5,8,1,128]{4,2,3,1,0:T(8,128)S(1)}, f32[2,5,8,1,128]{4,2,3,1,0:T(8,128)S(1)}, u32[]{:S(2)}, u32[]{:S(2)}) collective-permute-start(f32[2,5,8,1,128]{4,2,3,1,0:T(8,128)S(1)} %bitcast.62), channel_id=1, source_target_pairs={{1,0},{2,1},{3,2},{0,3},{5,4},{6,5},{7,6},{4,7},{9,8},{10,9},{11,1... | collective-permute-start | bytes 122888 | tf_op jit(solution)/shard_map/ppermute | solution.py:25
  57.1 9.1 %collective-permute-start.10 = (f32[2,5,1,10,128]{4,0,3,2,1:T(2,128)S(1)}, f32[2,5,1,10,128]{4,0,3,2,1:T(2,128)S(1)}, u32[]{:S(2)}, u32[]{:S(2)}) collective-permute-start(f32[2,5,1,10,128]{4,0,3,2,1:T(2,128)S(1)} %copy.356), channel_id=1, source_target_pairs={{0,4},{4,8},{8,12},{12,16},{16,20},{20,24},{24,28},{28,32},{32,36}... | collective-permute-start | bytes 153608 | tf_op jit(solution)/shard_map/ppermute | solution.py:22
  59.1 8.7 %collective-permute-start.11 = (f32[2,5,1,10,128]{4,0,3,2,1:T(2,128)S(1)}, f32[2,5,1,10,128]{4,0,3,2,1:T(2,128)S(1)}, u32[]{:S(2)}, u32[]{:S(2)}) collective-permute-start(f32[2,5,1,10,128]{4,0,3,2,1:T(2,128)S(1)} %copy.359), channel_id=1, source_target_pairs={{4,0},{8,4},{12,8},{16,12},{20,16},{24,20},{28,24},{32,28},{36,32}... | collective-permute-start | bytes 153608 | tf_op jit(solution)/shard_map/ppermute | solution.py:25
  68.3 0.7 copy-start.1
  86.4 9.0 %collective-permute-start.12 = (f32[2,1,120]{2,0,1:T(2,128)S(1)}, f32[2,1,120]{2,0,1:T(2,128)S(1)}, u32[]{:S(2)}, u32[]{:S(2)}) collective-permute-start(f32[2,1,120]{2,0,1:T(2,128)S(1)} %get-tuple-element.32), channel_id=1, source_target_pairs={{0,4},{4,8},{8,12},{12,16},{16,20},{20,24},{24,28},{28,32},{32,36}... | collective-permute-start | bytes 2888 | tf_op jit(solution)/shard_map/ppermute | solution.py:22
  88.3 8.2 %collective-permute-start.13 = (f32[2,1,120]{2,0,1:T(2,128)S(1)}, f32[2,1,120]{2,0,1:T(2,128)S(1)}, u32[]{:S(2)}, u32[]{:S(2)}) collective-permute-start(f32[2,1,120]{2,0,1:T(2,128)S(1)} %get-tuple-element.33), channel_id=1, source_target_pairs={{4,0},{8,4},{12,8},{16,12},{20,16},{24,20},{28,24},{32,28},{36,32}... | collective-permute-start | bytes 2888 | tf_op jit(solution)/shard_map/ppermute | solution.py:25
where the time goes:
time: 98.8 us; the launch traced here: 98.2 us
  starting transfers between devices  58.4 us (59%)
  blocking collectives  17.2 us (17%)
  waiting for transfers between devices  11.9 us (12%)
  local copies, waits for them, and re-layouts  6.2 us (6%)
  other arithmetic  2.42 us (2%)
  between operations  1.78 us (2%)
    ppermute x7, starting transfers between devices, padded(): lax.ppermute(lax.slice_in_dim(block, 0, width, axis=dim), axis, backward)  43.5 us
    unnamed x1, blocking collectives  17.2 us
    ppermute x7, starting transfers between devices, padded(): lax.ppermute(lax.slice_in_dim(block, block.shape[dim] - width, None, axis...  14.9 us
    ppermute x7, waiting for transfers between devices, padded(): lax.ppermute(lax.slice_in_dim(block, 0, width, axis=dim), axis, backward)  6.76 us
    ppermute x7, waiting for transfers between devices, padded(): lax.ppermute(lax.slice_in_dim(block, block.shape[dim] - width, None, axis...  5.16 us
  transfers between devices with their start and end apart: 14, of which 6 were waited for; matrix products, arithmetic and copies ran while one was open for 4% of the time, Pallas kernels for 0%

commit v1 on v0

v1 whole, which is shorter than its diff:
```python
import functools

import jax
import jax.numpy as jnp
import numpy as np
from jax import lax
from jax.experimental import pallas as pl
from jax.experimental.pallas import tpu as pltpu
from jax.sharding import PartitionSpec as P

NH = 48
NV = 5
WV = 2 * NV
ROWS = 8
NU = 0.15
section_weights = (1.0 / 3.0, 0.5, 1.0)
MESH = pl.DeviceIdType.MESH
HIGHEST = lax.Precision.HIGHEST
PEERS = [(db, dx) for db in (0, -1, 1) for dx in (0, 1, 3, 2) if (db, dx) != (0, 0)]


def harmonic_tables(slabs, slab):
    period = slabs * slab
    places = np.arange(period)[:, None]
    orders = np.arange(NH)[None, :]
    factor = np.where(orders == 0, 1.0, 2.0) / period
    cos_cols = np.cos(2.0 * np.pi * (places * orders % period) / period) * factor
    sin_cols = np.sin(2.0 * np.pi * (places * (orders + 1) % period) / period) * (2.0 / period)
    table = np.concatenate([cos_cols, sin_cols], 1)
    total = NV * 2 * NH
    chunk = total // slabs
    full = np.zeros((NV, period, total))
    for v in range(NV):
        full[v, :, v * 2 * NH:(v + 1) * 2 * NH] = table
    full = full.reshape(NV, slabs, slab, slabs, chunk).transpose(3, 1, 0, 2, 4)
    out = np.zeros((slabs, slabs, NV, slab, 128), np.float32)
    out[..., :chunk] = full
    return out


def kernel(blocks, slabs, speeds, states_hbm, steps_hbm, table_hbm, src_ref, frac_ref,
           out_ref, arr_ref,
           q0, dt, table, partial, field, send, halo, inter, inter_b, inter_c,
           load_sem, send_sem, recv_sem, isend_sem, irecv_sem):
    b = lax.axis_index("blk")
    x = lax.axis_index("pitch")

    def device(db, dx):
        return {"blk": lax.rem(b + db + blocks, blocks), "pitch": lax.rem(x + dx + slabs, slabs)}

    loads = [
        pltpu.make_async_copy(states_hbm, q0, load_sem.at[0]),
        pltpu.make_async_copy(steps_hbm, dt, load_sem.at[1]),
        pltpu.make_async_copy(table_hbm.at[x], table, load_sem.at[2]),
    ]
    for load in loads:
        load.start()
    barrier = pltpu.get_barrier_semaphore()
    for db, dx in PEERS:
        pl.semaphore_signal(barrier, inc=1, device_id=device(db, dx), device_id_type=MESH)

    lane = lax.broadcasted_iota(jnp.int32, (8, 128), 1)
    sub = lax.broadcasted_iota(jnp.int32, (8, 128), 0)
    low_edge = jnp.where(b == 0, 0.0, 1.0)
    high_edge = jnp.where(b == blocks - 1, 0.0, 1.0)

    def pack(source, stage):
        def body(i, carry):
            base = pl.multiple_of(i * 64, 64)
            send[stage, 0, i] = source[pl.ds(base + 7, 8, stride=8), :]
            send[stage, 1, i] = source[pl.ds(base, 8, stride=8), :]
            send[stage, 2, i] = source[pl.ds(base + 56, 8), :]
            send[stage, 3, i] = source[pl.ds(base, 8), :]
            return carry
        lax.fori_loop(0, WV, body, 0)

    def exchange(stage):
        copies = []
        for d, (db, dx) in enumerate(((0, 1), (0, -1), (1, 0), (-1, 0))):
            copies.append(pltpu.make_async_remote_copy(
                src_ref=send.at[stage, d], dst_ref=halo.at[stage, d],
                send_sem=send_sem.at[stage, d], recv_sem=recv_sem.at[stage, d],
                device_id=device(db, dx), device_id_type=MESH))
        return copies

    loads[0].wait()
    loads[1].wait()
    pack(q0, 0)
    chosen = []
    for w in range(2):
        first = 124 if w == 0 else -4
        pick = jnp.where((sub // 4 == w) & (lane == sub + first), 1.0, 0.0)
        cells = jnp.concatenate([q0[w * 320:(w + 1) * 320, :], dt[w * 64:(w + 1) * 64, :]], 0)
        chosen.append(lax.dot_general(pick, cells, (((1,), (1,)), ((), ())),
                                      precision=HIGHEST, preferred_element_type=jnp.float32))
    packet = chosen[0] + chosen[1]
    for j in range(3):
        inter[1, x, j] = packet[:, j * 128:(j + 1) * 128]

    pl.semaphore_wait(barrier, len(PEERS))
    stages = [exchange(stage) for stage in range(3)]
    for copy in stages[0]:
        copy.start()
    gathers = []
    for k, (db, dx) in enumerate(PEERS):
        gathers.append(pltpu.make_async_remote_copy(
            src_ref=inter.at[1, x], dst_ref=inter.at[1 - db, x],
            send_sem=isend_sem.at[k], recv_sem=irecv_sem.at[k],
            device_id=device(db, dx), device_id_type=MESH))
    for copy in gathers:
        copy.start()

    def inner(source, weight):
        def body(i, carry):
            base = pl.multiple_of(i * 64, 64)
            dbase = pl.multiple_of((i // NV) * 64, 64)
            a0, a1, a2 = speeds[i * 3], speeds[i * 3 + 1], speeds[i * 3 + 2]
            centre = -(a0 + a1 + a2) - 6.0 * NU
            axial_low = jnp.where(lane == 0, 0.0, a0 + NU)
            axial_high = jnp.where(lane == 127, 0.0, NU)
            pitch_low = jnp.where(sub == 0, 0.0, a2 + NU)
            pitch_high = jnp.where(sub == 7, 0.0, NU)
            rows = [source[pl.ds(base + r * 8, 8), :] for r in range(ROWS)]
            for r in range(ROWS):
                q = rows[r]
                total = centre * q
                total += axial_low * pltpu.roll(q, 1, 1)
                total += axial_high * pltpu.roll(q, 127, 1)
                total += pitch_low * pltpu.roll(q, 1, 0)
                total += pitch_high * pltpu.roll(q, 7, 0)
                if r > 0:
                    total += (a1 + NU) * rows[r - 1]
                if r < ROWS - 1:
                    total += NU * rows[r + 1]
                step = weight * dt[pl.ds(dbase + r * 8, 8), :]
                partial[pl.ds(base + r * 8, 8), :] = q0[pl.ds(base + r * 8, 8), :] + step * total
            return carry
        lax.fori_loop(0, WV, body, 0)

    def outer(stage, target, weight):
        def body(i, carry):
            base = pl.multiple_of(i * 64, 64)
            dbase = pl.multiple_of((i // NV) * 64, 64)
            a1, a2 = speeds[i * 3 + 1], speeds[i * 3 + 2]
            pitch_low = jnp.where(sub == 0, a2 + NU, 0.0)
            pitch_high = jnp.where(sub == 7, NU, 0.0)
            for r in range(ROWS):
                total = pitch_low * halo[stage, 0, i, pl.ds(r, 1), :]
                total += pitch_high * halo[stage, 1, i, pl.ds(r, 1), :]
                if r == 0:
                    total += (low_edge * (a1 + NU)) * halo[stage, 2, i]
                if r == ROWS - 1:
                    total += (high_edge * NU) * halo[stage, 3, i]
                step = weight * dt[pl.ds(dbase + r * 8, 8), :]
                target[pl.ds(base + r * 8, 8), :] = (
                    partial[pl.ds(base + r * 8, 8), :] + step * total)
            return carry
        lax.fori_loop(0, WV, body, 0)

    def speed_lanes(k, j):
        def of(w, v):
            return speeds[(w * NV + v) * 3 + k] if v < NV else 0.0
        return jnp.where(sub < 4,
                         jnp.where(lane < 64, of(0, 2 * j), of(0, 2 * j + 1)),
                         jnp.where(lane < 64, of(1, 2 * j), of(1, 2 * j + 1)))

    def interface_coefs():
        coefs = []
        for j in range(3):
            nu = NU if j < 2 else jnp.where(lane < 64, NU, 0.0)
            a0, a1, a2 = (speed_lanes(k, j) for k in range(3))
            coefs.append((-(a0 + a1 + a2) - 6.0 * nu,
                          jnp.where(sub == 4, 0.0, a0 + nu), jnp.where(sub == 3, 0.0, nu),
                          a1 + nu, nu, a2 + nu, nu))
        return coefs

    cell = lax.rem(lane, 8)
    row = lax.rem(lane, 64) // 8

    def interface_section(source, weight, coefs, s):
        before = lax.rem(s + slabs - 1, slabs)
        after = lax.rem(s + 1, slabs)
        result = []
        for d in range(3):
            last = inter[d, s, 2]
            step = weight * jnp.where(lane < 64, pltpu.roll(last, 64, 1), last)
            parts = []
            for j in range(3):
                c, xl, xh, rl, rh, pl_, ph = coefs[j]
                q = source[d, s, j]
                total = c * q + xl * pltpu.roll(q, 1, 0) + xh * pltpu.roll(q, 7, 0)
                total += pl_ * jnp.where(cell == 0, pltpu.roll(source[d, before, j], 121, 1),
                                         pltpu.roll(q, 1, 1))
                total += ph * jnp.where(cell == 7, pltpu.roll(source[d, after, j], 7, 1),
                                        pltpu.roll(q, 127, 1))
                low = pltpu.roll(q, 8, 1)
                if d > 0:
                    low = jnp.where(row == 0, pltpu.roll(source[d - 1, s, j], 72, 1), low)
                high = pltpu.roll(q, 120, 1)
                if d < 2:
                    high = jnp.where(row == 7, pltpu.roll(source[d + 1, s, j], 56, 1), high)
                total += rl * low + rh * high
                parts.append(inter[d, s, j] + step * total)
            result.append(parts)
        return result

    def interface_step(source, target, weight):
        def body(s, carry):
            coefs = interface_coefs()
            result = interface_section(source, weight, coefs, s)
            for d in range(3):
                for j in range(3):
                    target[d, s, j] = result[d][j]
            return carry
        lax.fori_loop(0, slabs, body, 0)

    def interface_last(source, weight):
        shares = []
        for w in range(2):
            per_block = []
            for d in range(3):
                place = (b + d - 1) * ROWS + row
                share = jnp.zeros((8, 128), jnp.float32)
                for slot in range(3):
                    share += jnp.where(src_ref[w, :, slot:slot + 1] == place,
                                       frac_ref[w, :, slot:slot + 1].astype(jnp.float32)
                                       * (1.0 / 65536.0), 0.0)
                per_block.append(share)
            shares.append(per_block)

        def body(s, total):
            coefs = interface_coefs()
            result = interface_section(source, weight, coefs, s)
            sides = []
            for w in range(2):
                at = 4 if w == 0 else 3
                columns = []
                for j in range(3):
                    columns.append(sum(jnp.broadcast_to(result[d][j][at:at + 1, :], (8, 128))
                                       * shares[w][d] for d in range(3)))
                sides.append(jnp.concatenate(columns, 1))
            lhs = jnp.concatenate(sides, 0)
            waves = []
            for v in range(NV):
                waves += [table[s, v]] * ROWS
            waves.append(jnp.zeros((64, 128), jnp.float32))
            rhs = jnp.concatenate(waves, 0)
            return total + jnp.dot(lhs, rhs, precision=HIGHEST,
                                   preferred_element_type=jnp.float32)
        total = lax.fori_loop(0, slabs, body, jnp.zeros((16, 128), jnp.float32))
        columns = arr_ref.shape[2]
        arr_ref[0] = total[0:8, 0:columns]
        arr_ref[1] = total[8:16, 0:columns]

    w1, w2, w3 = section_weights
    inner(q0, w1)
    for copy in stages[0]:
        copy.wait_recv()
    outer(0, field, w1)
    pack(field, 1)
    for copy in stages[1]:
        copy.start()

    inner(field, w2)
    for copy in gathers:
        copy.wait_send()
    for copy in gathers:
        copy.wait_recv()

    def edges(s, carry):
        for j in range(3):
            inter[0, s, j] = inter[0, s, j] * low_edge
            inter[2, s, j] = inter[2, s, j] * high_edge
        return carry
    lax.fori_loop(0, slabs, edges, 0)
    interface_step(inter, inter_b, w1)
    for copy in stages[1]:
        copy.wait_recv()
    outer(1, field, w2)
    pack(field, 2)
    for copy in stages[2]:
        copy.start()

    inner(field, w3)
    interface_step(inter_b, inter_c, w2)
    loads[2].wait()
    interface_last(inter_c, w3)
    for copy in stages[2]:
        copy.wait_recv()
    outer(2, out_ref, w3)
    for stage in stages:
        for copy in stage:
            copy.wait_send()


def shards(tables, states, time_steps, speeds, band_src, band_frac):
    blocks = lax.axis_size("blk")
    slabs = lax.axis_size("pitch")
    any_space = pl.BlockSpec(memory_space=pl.ANY)
    vmem = pl.BlockSpec(memory_space=pltpu.VMEM)
    cells = WV * ROWS * 8
    columns = NV * 2 * NH // slabs
    field, arrivals = pl.pallas_call(
        functools.partial(kernel, blocks, slabs),
        out_shape=(jax.ShapeDtypeStruct((cells, 128), jnp.float32),
                   jax.ShapeDtypeStruct((2, ROWS, columns), jnp.float32)),
        in_specs=[pl.BlockSpec(memory_space=pltpu.SMEM), any_space, any_space, any_space,
                  vmem, vmem],
        out_specs=(vmem, vmem),
        scratch_shapes=[
            pltpu.VMEM((cells, 128), jnp.float32),
            pltpu.VMEM((128, 128), jnp.float32),
            pltpu.VMEM((slabs, NV, 8, 128), jnp.float32),
            pltpu.VMEM((cells, 128), jnp.float32),
            pltpu.VMEM((cells, 128), jnp.float32),
            pltpu.VMEM((3, 4, WV, 8, 128), jnp.float32),
            pltpu.VMEM((3, 4, WV, 8, 128), jnp.float32),
            pltpu.VMEM((3, slabs, 3, 8, 128), jnp.float32),
            pltpu.VMEM((3, slabs, 3, 8, 128), jnp.float32),
            pltpu.VMEM((3, slabs, 3, 8, 128), jnp.float32),
            pltpu.SemaphoreType.DMA((3,)),
            pltpu.SemaphoreType.DMA((3, 4)),
            pltpu.SemaphoreType.DMA((3, 4)),
            pltpu.SemaphoreType.DMA((len(PEERS),)),
            pltpu.SemaphoreType.DMA((len(PEERS),)),
        ],
        compiler_params=pltpu.CompilerParams(collective_id=0, has_side_effects=True),
        name="window",
    )(speeds.reshape(-1), states.reshape(cells, 128), time_steps.reshape(128, 128),
      jnp.asarray(tables), band_src, band_frac)
    return field.reshape(states.shape), arrivals


def solution(mesh):
    tables = harmonic_tables(mesh.shape["pitch"], 8)
    return jax.shard_map(
        functools.partial(shards, tables),
        mesh=mesh,
        in_specs=(
            P(None, None, "blk", "pitch", None),
            P(None, "blk", "pitch", None),
            P(),
            P(None, "blk", None),
            P(None, "blk", None),
        ),
        out_specs=(P(None, None, "blk", "pitch", None), P(None, "blk", "pitch")),
        check_vma=False,
    )
```

time: 98.8 us -> 34.3 us (0.35)
  the two profiles are of different devices: /device:TPU:32 before, /device:TPU:2 now
where the time goes in v1:
time: 34.3 us; the launch traced here: 34 us
  Pallas kernels  28.2 us (82%)
  local copies, waits for them, and re-layouts  5.16 us (15%)
  between operations  0.66 us (2%)
    pallas_call x1, Pallas kernels, shards(): pl.pallas_call(functools.partial(kernel, blocks, slabs), out_shape=(jax.S...  28.2 us
    unnamed x13, local copies, waits for them, and re-layouts  4.48 us

profile of v1, /device:TPU:2, one launch (start us, length us, event | category | flops | bytes accessed | tf_op | source)
XLA Modules:
  0.0 34.0 jit_solution(4761735834886335268)
XLA Ops:
  0.6 0.0 copy-start.1
  0.6 0.7 %copy-done.1 = f32[2,5,3]{1,0,2:T(2,128)S(1)} copy-done((f32[2,5,3]{1,0,2:T(2,128)S(1)}, f32[2,5,3]{1,0,2:T(2,128)}, u32[]{:S(2)}) %copy-start.1) | copy-done | bytes 144
  1.3 0.1 copy.11
  1.4 0.0 copy-start.2
  1.4 0.7 %reshape.16.speeds = f32[30]{0:T(128)} reshape(f32[2,5,3]{2,1,0:T(8,128)S(1)} %copy.11) | data formatting | bytes 240 | tf_op jit(solution)/shard_map/reshape | solution.py:329
  2.1 0.0 copy-done.2
  2.1 0.0 copy-start.3
  2.1 0.7 %copy.12.src_ref = s32[2,8,3]{2,1,0:T(8,128)} copy(s32[2,8,3]{1,0,2:T(2,128)S(1)} %copy-done.2) | data formatting | bytes 384 | tf_op args[3]
  2.8 0.0 copy-done.3
  2.8 0.7 %copy.13.frac_ref = s32[2,8,3]{2,1,0:T(8,128)} copy(s32[2,8,3]{1,0,2:T(2,128)S(1)} %copy-done.3) | data formatting | bytes 384 | tf_op args[4]
  3.5 28.2 %window.1 = (f32[640,128]{1,0:T(8,128)}, f32[2,8,120]{2,1,0:T(8,128)}) custom-call(f32[30]{0:T(128)} %reshape.16.speeds, f32[640,128]{1,0:T(8,128)} %bitcast.3, f32[128,128]{1,0:T(8,128)} %bitcast.5, f32[4,4,5,8,128]{4,3,2,1,0:T(8,128)} %constant.2.clone.table_hbm, s32[2,8,3]{2,1,0:T(8,128)} %copy.12.src_ref, s32[2,8,3]{2,1,0:T(8,128)} %copy.13.frac_ref), custom_call_target="tpu_custom_call" | custom-call | tf_op jit(solution)/shard_map/window/pallas_call | solution.py:303
  31.7 0.0 copy-start
  31.7 1.7 %copy.16 = f32[2,5,8,8,128]{4,3,2,1,0:T(8,128)} copy(f32[2,5,8,8,128]{4,3,2,1,0:T(8,128)} %bitcast.4) | data formatting | bytes 655360
  33.4 0.0 copy-done
  33.4 0.6 %copy.17 = f32[2,8,120]{2,1,0:T(8,128)} copy(f32[2,8,120]{2,1,0:T(8,128)S(1)} %copy-done) | data formatting | bytes 15360
Async XLA Ops:
  0.6 0.7 %copy-start.1 = (f32[2,5,3]{1,0,2:T(2,128)S(1)}, f32[2,5,3]{1,0,2:T(2,128)}, u32[]{:S(2)}) copy-start(f32[2,5,3]{1,0,2:T(2,128)} %param.8) | copy-start | bytes 364
  1.4 0.7 %copy-start.2 = (s32[2,8,3]{1,0,2:T(2,128)S(1)}, s32[2,8,3]{1,0,2:T(2,128)}, u32[]{:S(2)}) copy-start(s32[2,8,3]{1,0,2:T(2,128)} %param.9) | copy-start | bytes 580
  2.1 0.7 %copy-start.3 = (s32[2,8,3]{1,0,2:T(2,128)S(1)}, s32[2,8,3]{1,0,2:T(2,128)}, u32[]{:S(2)}) copy-start(s32[2,8,3]{1,0,2:T(2,128)} %param.10) | copy-start | bytes 580
  31.7 1.7 %copy-start = (f32[2,8,120]{2,1,0:T(8,128)S(1)}, f32[2,8,120]{2,1,0:T(8,128)}, u32[]{:S(2)}) copy-start(f32[2,8,120]{2,1,0:T(8,128)} %get-tuple-element.9) | copy-start | bytes 23044

commit v2 on v1

--- a/solution.py
+++ b/solution.py
@@ -38,9 +38,9 @@
     return out
 
 
-def kernel(blocks, slabs, speeds, states_hbm, steps_hbm, table_hbm, src_ref, frac_ref,
+def kernel(blocks, slabs, speeds_hbm, states_hbm, steps_hbm, table_hbm, src_hbm, frac_hbm,
            out_ref, arr_ref,
-           q0, dt, table, partial, field, send, halo, inter, inter_b, inter_c,
+           speeds, src_ref, frac_ref, q0, dt, table, partial, field, send, halo, inter, inter_b, inter_c,
            load_sem, send_sem, recv_sem, isend_sem, irecv_sem):
     b = lax.axis_index("blk")
     x = lax.axis_index("pitch")
@@ -48,16 +48,19 @@
     def device(db, dx):
         return {"blk": lax.rem(b + db + blocks, blocks), "pitch": lax.rem(x + dx + slabs, slabs)}
 
+    barrier = pltpu.get_barrier_semaphore()
+    for db, dx in PEERS:
+        pl.semaphore_signal(barrier, inc=1, device_id=device(db, dx), device_id_type=MESH)
     loads = [
         pltpu.make_async_copy(states_hbm, q0, load_sem.at[0]),
         pltpu.make_async_copy(steps_hbm, dt, load_sem.at[1]),
         pltpu.make_async_copy(table_hbm.at[x], table, load_sem.at[2]),
+        pltpu.make_async_copy(speeds_hbm, speeds, load_sem.at[3]),
+        pltpu.make_async_copy(src_hbm, src_ref, load_sem.at[4]),
+        pltpu.make_async_copy(frac_hbm, frac_ref, load_sem.at[5]),
     ]
     for load in loads:
         load.start()
-    barrier = pltpu.get_barrier_semaphore()
-    for db, dx in PEERS:
-        pl.semaphore_signal(barrier, inc=1, device_id=device(db, dx), device_id_type=MESH)
 
     lane = lax.broadcasted_iota(jnp.int32, (8, 128), 1)
     sub = lax.broadcasted_iota(jnp.int32, (8, 128), 0)
@@ -114,7 +117,7 @@
         def body(i, carry):
             base = pl.multiple_of(i * 64, 64)
             dbase = pl.multiple_of((i // NV) * 64, 64)
-            a0, a1, a2 = speeds[i * 3], speeds[i * 3 + 1], speeds[i * 3 + 2]
+            a0, a1, a2 = (speeds[k, i // NV, lax.rem(i, NV)] for k in range(3))
             centre = -(a0 + a1 + a2) - 6.0 * NU
             axial_low = jnp.where(lane == 0, 0.0, a0 + NU)
             axial_high = jnp.where(lane == 127, 0.0, NU)
@@ -141,7 +144,7 @@
         def body(i, carry):
             base = pl.multiple_of(i * 64, 64)
             dbase = pl.multiple_of((i // NV) * 64, 64)
-            a1, a2 = speeds[i * 3 + 1], speeds[i * 3 + 2]
+            a1, a2 = (speeds[k, i // NV, lax.rem(i, NV)] for k in range(1, 3))
             pitch_low = jnp.where(sub == 0, a2 + NU, 0.0)
             pitch_high = jnp.where(sub == 7, NU, 0.0)
             for r in range(ROWS):
@@ -159,7 +162,7 @@
 
     def speed_lanes(k, j):
         def of(w, v):
-            return speeds[(w * NV + v) * 3 + k] if v < NV else 0.0
+            return speeds[k, w, v] if v < NV else 0.0
         return jnp.where(sub < 4,
                          jnp.where(lane < 64, of(0, 2 * j), of(0, 2 * j + 1)),
                          jnp.where(lane < 64, of(1, 2 * j), of(1, 2 * j + 1)))
@@ -215,16 +218,22 @@
         lax.fori_loop(0, slabs, body, 0)
 
     def interface_last(source, weight):
+        near = (lax.broadcasted_iota(jnp.int32, (8, 8), 0)
+                == lax.broadcasted_iota(jnp.int32, (8, 8), 1))
+
+        def column(ref, slot, w):
+            line = jnp.broadcast_to(ref[slot, w:w + 1, :].astype(jnp.float32), (8, 8))
+            return jnp.sum(jnp.where(near, line, 0.0), axis=1, keepdims=True)
+        columns_of = [[(column(src_ref, slot, w), column(frac_ref, slot, w) * (1.0 / 65536.0))
+                       for slot in range(3)] for w in range(2)]
         shares = []
         for w in range(2):
             per_block = []
             for d in range(3):
-                place = (b + d - 1) * ROWS + row
+                place = ((b + d - 1) * ROWS + row).astype(jnp.float32)
                 share = jnp.zeros((8, 128), jnp.float32)
-                for slot in range(3):
-                    share += jnp.where(src_ref[w, :, slot:slot + 1] == place,
-                                       frac_ref[w, :, slot:slot + 1].astype(jnp.float32)
-                                       * (1.0 / 65536.0), 0.0)
+                for origin, fraction in columns_of[w]:
+                    share += jnp.where(origin == place, fraction, 0.0)
                 per_block.append(share)
             shares.append(per_block)
 
@@ -253,6 +262,7 @@
         arr_ref[1] = total[8:16, 0:columns]
 
     w1, w2, w3 = section_weights
+    loads[3].wait()
     inner(q0, w1)
     for copy in stages[0]:
         copy.wait_recv()
@@ -283,7 +293,8 @@
 
     inner(field, w3)
     interface_step(inter_b, inter_c, w2)
-    loads[2].wait()
+    for load in (loads[2], loads[4], loads[5]):
+        load.wait()
     interface_last(inter_c, w3)
     for copy in stages[2]:
         copy.wait_recv()
@@ -302,12 +313,14 @@
     columns = NV * 2 * NH // slabs
     field, arrivals = pl.pallas_call(
         functools.partial(kernel, blocks, slabs),
-        out_shape=(jax.ShapeDtypeStruct((cells, 128), jnp.float32),
-                   jax.ShapeDtypeStruct((2, ROWS, columns), jnp.float32)),
-        in_specs=[pl.BlockSpec(memory_space=pltpu.SMEM), any_space, any_space, any_space,
-                  vmem, vmem],
+        out_shape=(pltpu.VMEM((cells, 128), jnp.float32),
+                   pltpu.VMEM((2, ROWS, columns), jnp.float32)),
+        in_specs=[any_space] * 6,
         out_specs=(vmem, vmem),
         scratch_shapes=[
+            pltpu.SMEM((3, 2, NV), jnp.float32),
+            pltpu.VMEM((3, 2, ROWS), jnp.int32),
+            pltpu.VMEM((3, 2, ROWS), jnp.int32),
             pltpu.VMEM((cells, 128), jnp.float32),
             pltpu.VMEM((128, 128), jnp.float32),
             pltpu.VMEM((slabs, NV, 8, 128), jnp.float32),
@@ -318,7 +331,7 @@
             pltpu.VMEM((3, slabs, 3, 8, 128), jnp.float32),
             pltpu.VMEM((3, slabs, 3, 8, 128), jnp.float32),
             pltpu.VMEM((3, slabs, 3, 8, 128), jnp.float32),
-            pltpu.SemaphoreType.DMA((3,)),
+            pltpu.SemaphoreType.DMA((6,)),
             pltpu.SemaphoreType.DMA((3, 4)),
             pltpu.SemaphoreType.DMA((3, 4)),
             pltpu.SemaphoreType.DMA((len(PEERS),)),
@@ -326,8 +339,8 @@
         ],
         compiler_params=pltpu.CompilerParams(collective_id=0, has_side_effects=True),
         name="window",
-    )(speeds.reshape(-1), states.reshape(cells, 128), time_steps.reshape(128, 128),
-      jnp.asarray(tables), band_src, band_frac)
+    )(jnp.transpose(speeds, (2, 0, 1)), states.reshape(cells, 128), time_steps.reshape(128, 128),
+      jnp.asarray(tables), jnp.transpose(band_src, (2, 0, 1)), jnp.transpose(band_frac, (2, 0, 1)))
     return field.reshape(states.shape), arrivals
 
 

time: 34.3 us -> 29.1 us (0.85)
  local copies, waits for them, and re-layouts: 5.16 us -> 1.32 us
  Pallas kernels: 28.2 us -> 27 us
    unnamed x13 -> x2, local copies, waits for them, and re-layouts: 4.48 us -> 1.32 us
    pallas_call x1, Pallas kernels: 28.2 us -> 27 us  [shards(): pl.pallas_call(functools.partial(kernel, blocks, slabs), out_shape=(pltpu...]
    reshape x1 -> x0, local copies, waits for them, and re-layouts: 0.68 us -> none  [shards(): speeds.reshape(-1)]
where the time goes in v2:
time: 29.1 us; the launch traced here: 29 us
  Pallas kernels  27 us (93%)
  local copies, waits for them, and re-layouts  1.32 us (5%)
  between operations  0.64 us (2%)
    pallas_call x1, Pallas kernels, shards(): pl.pallas_call(functools.partial(kernel, blocks, slabs), out_shape=(pltpu...  27 us
    unnamed x2, local copies, waits for them, and re-layouts  1.32 us

profile of v2, /device:TPU:2, one launch (start us, length us, event | category | flops | bytes accessed | tf_op | source)
XLA Modules:
  0.0 29.0 jit_solution(1663236315874582502)
XLA Ops:
  0.6 27.0 %window.1 = (f32[640,128]{1,0:T(8,128)S(1)}, f32[2,8,120]{2,1,0:T(8,128)S(1)}) custom-call(f32[3,2,5]{2,1,0:T(2,128)} %bitcast.9, f32[640,128]{1,0:T(8,128)} %bitcast.7, f32[128,128]{1,0:T(8,128)} %bitcast.8, f32[4,4,5,8,128]{4,3,2,1,0:T(8,128)} %constant.2.clone.table_hbm, s32[3,2,8]{2,1,0:T(2,128)} %bitcast.10, s32[3,2,8]{2,1,0:T(2,128)} %bitcast.11), custom_call_target="tpu_custom_call" | custom-call | tf_op jit(solution)/shard_map/window/pallas_call | solution.py:314
  27.6 0.7 %copy.10 = f32[2,5,8,8,128]{4,3,2,1,0:T(8,128)} copy(f32[2,5,8,8,128]{4,3,2,1,0:T(8,128)S(1)} %bitcast.6) | data formatting | bytes 655360
  28.4 0.6 %copy.11 = f32[2,8,120]{2,1,0:T(8,128)} copy(f32[2,8,120]{2,1,0:T(8,128)S(1)} %get-tuple-element.7) | data formatting | bytes 15360

commit v3 on v2

--- a/solution.py
+++ b/solution.py
@@ -49,8 +49,19 @@
         return {"blk": lax.rem(b + db + blocks, blocks), "pitch": lax.rem(x + dx + slabs, slabs)}
 
     barrier = pltpu.get_barrier_semaphore()
-    for db, dx in PEERS:
-        pl.semaphore_signal(barrier, inc=1, device_id=device(db, dx), device_id_type=MESH)
+
+    def where_blocks(db, action):
+        if db == 0:
+            action()
+        else:
+            pl.when(b > 0 if db < 0 else b < blocks - 1)(action)
+
+    def greet(db):
+        for peer in PEERS:
+            if peer[0] == db:
+                pl.semaphore_signal(barrier, inc=1, device_id=device(*peer), device_id_type=MESH)
+    for db in (0, -1, 1):
+        where_blocks(db, functools.partial(greet, db))
     loads = [
         pltpu.make_async_copy(states_hbm, q0, load_sem.at[0]),
         pltpu.make_async_copy(steps_hbm, dt, load_sem.at[1]),
@@ -64,31 +75,62 @@
 
     lane = lax.broadcasted_iota(jnp.int32, (8, 128), 1)
     sub = lax.broadcasted_iota(jnp.int32, (8, 128), 0)
-    low_edge = jnp.where(b == 0, 0.0, 1.0)
-    high_edge = jnp.where(b == blocks - 1, 0.0, 1.0)
-
-    def pack(source, stage):
-        def body(i, carry):
-            base = pl.multiple_of(i * 64, 64)
-            send[stage, 0, i] = source[pl.ds(base + 7, 8, stride=8), :]
-            send[stage, 1, i] = source[pl.ds(base, 8, stride=8), :]
-            send[stage, 2, i] = source[pl.ds(base + 56, 8), :]
-            send[stage, 3, i] = source[pl.ds(base, 8), :]
-            return carry
-        lax.fori_loop(0, WV, body, 0)
+
+    @pl.when(b == 0)
+    def _():
+        for stage in range(3):
+            halo[stage, 2] = jnp.zeros((WV, 8, 128), jnp.float32)
+        inter[0] = jnp.zeros(inter.shape[1:], jnp.float32)
+
+    @pl.when(b == blocks - 1)
+    def _():
+        for stage in range(3):
+            halo[stage, 3] = jnp.zeros((WV, 8, 128), jnp.float32)
+        inter[2] = jnp.zeros(inter.shape[1:], jnp.float32)
+
+    def pack(source, stage, i):
+        base = pl.multiple_of(i * 64, 64)
+        send[stage, 0, i] = source[pl.ds(base + 7, 8, stride=8), :]
+        send[stage, 1, i] = source[pl.ds(base, 8, stride=8), :]
+        send[stage, 2, i] = source[pl.ds(base + 56, 8), :]
+        send[stage, 3, i] = source[pl.ds(base, 8), :]
 
     def exchange(stage):
         copies = []
         for d, (db, dx) in enumerate(((0, 1), (0, -1), (1, 0), (-1, 0))):
-            copies.append(pltpu.make_async_remote_copy(
+            copies.append((db, pltpu.make_async_remote_copy(
                 src_ref=send.at[stage, d], dst_ref=halo.at[stage, d],
                 send_sem=send_sem.at[stage, d], recv_sem=recv_sem.at[stage, d],
-                device_id=device(db, dx), device_id_type=MESH))
+                device_id=device(db, dx), device_id_type=MESH)))
         return copies
+
+    def start(copies):
+        for sign in (1, -1, 0):
+            chosen = [copy for db, copy in copies if db == sign]
+            where_blocks(sign, lambda: [copy.start() for copy in chosen] and None)
+
+    def wait_recv(copies):
+        for sign in (0, 1, -1):
+            chosen = [copy for db, copy in copies if db == sign]
+            where_blocks(-sign, lambda: [copy.wait_recv() for copy in chosen] and None)
+
+    def wait_send(copies):
+        for sign in (0, 1, -1):
+            chosen = [copy for db, copy in copies if db == sign]
+            where_blocks(sign, lambda: [copy.wait_send() for copy in chosen] and None)
 
     loads[0].wait()
     loads[1].wait()
-    pack(q0, 0)
+
+    def pack_body(i, carry):
+        pack(q0, 0, i)
+        return carry
+    lax.fori_loop(0, WV, pack_body, 0)
+    below = (b + blocks - 1) // blocks
+    above = (2 * blocks - 2 - b) // blocks
+    pl.semaphore_wait(barrier, slabs - 1 + slabs * (below + above))
+    stages = [exchange(stage) for stage in range(3)]
+    start(stages[0])
     chosen = []
     for w in range(2):
         first = 124 if w == 0 else -4
@@ -100,18 +142,13 @@
     for j in range(3):
         inter[1, x, j] = packet[:, j * 128:(j + 1) * 128]
 
-    pl.semaphore_wait(barrier, len(PEERS))
-    stages = [exchange(stage) for stage in range(3)]
-    for copy in stages[0]:
-        copy.start()
     gathers = []
     for k, (db, dx) in enumerate(PEERS):
-        gathers.append(pltpu.make_async_remote_copy(
+        gathers.append((db, pltpu.make_async_remote_copy(
             src_ref=inter.at[1, x], dst_ref=inter.at[1 - db, x],
             send_sem=isend_sem.at[k], recv_sem=irecv_sem.at[k],
-            device_id=device(db, dx), device_id_type=MESH))
-    for copy in gathers:
-        copy.start()
+            device_id=device(db, dx), device_id_type=MESH)))
+    start(gathers)
 
     def inner(source, weight):
         def body(i, carry):
@@ -151,12 +188,14 @@
                 total = pitch_low * halo[stage, 0, i, pl.ds(r, 1), :]
                 total += pitch_high * halo[stage, 1, i, pl.ds(r, 1), :]
                 if r == 0:
-                    total += (low_edge * (a1 + NU)) * halo[stage, 2, i]
+                    total += (a1 + NU) * halo[stage, 2, i]
                 if r == ROWS - 1:
-                    total += (high_edge * NU) * halo[stage, 3, i]
+                    total += NU * halo[stage, 3, i]
                 step = weight * dt[pl.ds(dbase + r * 8, 8), :]
                 target[pl.ds(base + r * 8, 8), :] = (
                     partial[pl.ds(base + r * 8, 8), :] + step * total)
+            if stage < 2:
+                pack(target, stage + 1, i)
             return carry
         lax.fori_loop(0, WV, body, 0)
 
@@ -264,44 +303,40 @@
     w1, w2, w3 = section_weights
     loads[3].wait()
     inner(q0, w1)
-    for copy in stages[0]:
-        copy.wait_recv()
+    wait_recv(stages[0])
     outer(0, field, w1)
-    pack(field, 1)
-    for copy in stages[1]:
-        copy.start()
+    start(stages[1])
 
     inner(field, w2)
-    for copy in gathers:
-        copy.wait_send()
-    for copy in gathers:
-        copy.wait_recv()
-
-    def edges(s, carry):
-        for j in range(3):
-            inter[0, s, j] = inter[0, s, j] * low_edge
-            inter[2, s, j] = inter[2, s, j] * high_edge
-        return carry
-    lax.fori_loop(0, slabs, edges, 0)
+    wait_recv(gathers)
     interface_step(inter, inter_b, w1)
-    for copy in stages[1]:
-        copy.wait_recv()
+    wait_recv(stages[1])
     outer(1, field, w2)
-    pack(field, 2)
-    for copy in stages[2]:
-        copy.start()
+    start(stages[2])
 
     inner(field, w3)
     interface_step(inter_b, inter_c, w2)
     for load in (loads[2], loads[4], loads[5]):
         load.wait()
     interface_last(inter_c, w3)
-    for copy in stages[2]:
-        copy.wait_recv()
+    wait_send(gathers)
+    for stage in stages[:2]:
+        wait_send(stage)
+    wait_recv(stages[2])
     outer(2, out_ref, w3)
-    for stage in stages:
-        for copy in stage:
-            copy.wait_send()
+    wait_send(stages[2])
+
+
+def write_out(field_ref, arr_ref, field_hbm, arr_hbm, sems):
+    quarter = field_ref.shape[0] // 4
+    copies = [pltpu.make_async_copy(field_ref.at[pl.ds(k * quarter, quarter)],
+                                    field_hbm.at[pl.ds(k * quarter, quarter)], sems.at[k])
+              for k in range(4)]
+    copies.append(pltpu.make_async_copy(arr_ref, arr_hbm, sems.at[4]))
+    for copy in copies:
+        copy.start()
+    for copy in copies:
+        copy.wait()
 
 
 def shards(tables, states, time_steps, speeds, band_src, band_frac):
@@ -341,6 +376,16 @@
         name="window",
     )(jnp.transpose(speeds, (2, 0, 1)), states.reshape(cells, 128), time_steps.reshape(128, 128),
       jnp.asarray(tables), jnp.transpose(band_src, (2, 0, 1)), jnp.transpose(band_frac, (2, 0, 1)))
+    field, arrivals = pl.pallas_call(
+        write_out,
+        out_shape=(jax.ShapeDtypeStruct(field.shape, jnp.float32),
+                   jax.ShapeDtypeStruct(arrivals.shape, jnp.float32)),
+        in_specs=[vmem] * 2,
+        out_specs=(any_space, any_space),
+        scratch_shapes=[pltpu.SemaphoreType.DMA((5,))],
+        name="write_out",
+    )(pltpu.with_memory_space_constraint(field, pltpu.VMEM),
+      pltpu.with_memory_space_constraint(arrivals, pltpu.VMEM))
     return field.reshape(states.shape), arrivals
 
 

time: 29.1 us -> 26 us (0.89)
  the two profiles are of different devices: /device:TPU:2 before, /device:TPU:32 now
where the time goes in v3:
time: 26 us; the launch traced here: 25.9 us
  Pallas kernels  25.2 us (97%)
  between operations  0.64 us (2%)
    pallas_call x1, Pallas kernels, shards(): pl.pallas_call(functools.partial(kernel, blocks, slabs), out_shape=(pltpu...  24.5 us
    pallas_call x1, Pallas kernels, shards(): pl.pallas_call(write_out, out_shape=(jax.ShapeDtypeStruct(field.shape, jn...  0.77 us

profile of v3, /device:TPU:32, one launch (start us, length us, event | category | flops | bytes accessed | tf_op | source)
XLA Modules:
  0.0 25.9 jit_solution(6977929677518916575)
XLA Ops:
  0.6 24.5 %window.1 = (f32[640,128]{1,0:T(8,128)S(1)}, f32[2,8,120]{2,1,0:T(8,128)S(1)}) custom-call(f32[3,2,5]{2,1,0:T(2,128)} %bitcast.8, f32[640,128]{1,0:T(8,128)} %bitcast.6, f32[128,128]{1,0:T(8,128)} %bitcast.7, f32[4,4,5,8,128]{4,3,2,1,0:T(8,128)} %constant.2.clone.table_hbm, s32[3,2,8]{2,1,0:T(2,128)} %bitcast.9, s32[3,2,8]{2,1,0:T(2,128)} %bitcast.10), custom_call_target="tpu_custom_call" | custom-call | tf_op jit(solution)/shard_map/window/pallas_call | solution.py:349
  25.1 0.8 %write_out.1 = (f32[640,128]{1,0:T(8,128)}, f32[2,8,120]{2,1,0:T(8,128)}) custom-call(f32[640,128]{1,0:T(8,128)S(1)} %get-tuple-element.6.field_ref, f32[2,8,120]{2,1,0:T(8,128)S(1)} %get-tuple-element.7.arr_ref), custom_call_target="tpu_custom_call" | custom-call | tf_op jit(solution)/shard_map/write_out/pallas_call | solution.py:379

commit v4 on v3

--- a/solution.py
+++ b/solution.py
@@ -16,7 +16,10 @@
 section_weights = (1.0 / 3.0, 0.5, 1.0)
 MESH = pl.DeviceIdType.MESH
 HIGHEST = lax.Precision.HIGHEST
-PEERS = [(db, dx) for db in (0, -1, 1) for dx in (0, 1, 3, 2) if (db, dx) != (0, 0)]
+NEAR = ((0, 1), (0, -1), (1, 0), (-1, 0))
+RELAYS = (((0, 1, 0), (0, -1, 0), (0, 0, 1), (0, 0, -1)),
+          ((-1, 0, 1), (-1, 1, 0), (-1, -1, 0), (1, 1, 0), (1, -1, 0)),
+          ((2, 1, 0), (2, -1, 0)))
 
 
 def harmonic_tables(slabs, slab):
@@ -38,7 +41,7 @@
     return out
 
 
-def kernel(blocks, slabs, speeds_hbm, states_hbm, steps_hbm, table_hbm, src_hbm, frac_hbm,
+def kernel(blocks, slabs, speeds_hbm, blocks_hbm, states_hbm, steps_hbm, table_hbm, src_hbm, frac_hbm,
            out_ref, arr_ref,
            speeds, src_ref, frac_ref, q0, dt, table, partial, field, send, halo, inter, inter_b, inter_c,
            load_sem, send_sem, recv_sem, isend_sem, irecv_sem):
@@ -57,7 +60,7 @@
             pl.when(b > 0 if db < 0 else b < blocks - 1)(action)
 
     def greet(db):
-        for peer in PEERS:
+        for peer in NEAR:
             if peer[0] == db:
                 pl.semaphore_signal(barrier, inc=1, device_id=device(*peer), device_id_type=MESH)
     for db in (0, -1, 1):
@@ -95,11 +98,14 @@
         send[stage, 2, i] = source[pl.ds(base + 56, 8), :]
         send[stage, 3, i] = source[pl.ds(base, 8), :]
 
+    faces = (blocks_hbm.at[:, :, 7], blocks_hbm.at[:, :, 0],
+             blocks_hbm.at[:, ROWS - 1], blocks_hbm.at[:, 0])
+
     def exchange(stage):
         copies = []
-        for d, (db, dx) in enumerate(((0, 1), (0, -1), (1, 0), (-1, 0))):
+        for d, (db, dx) in enumerate(NEAR):
             copies.append((db, pltpu.make_async_remote_copy(
-                src_ref=send.at[stage, d], dst_ref=halo.at[stage, d],
+                src_ref=faces[d] if stage == 0 else send.at[stage - 1, d], dst_ref=halo.at[stage, d],
                 send_sem=send_sem.at[stage, d], recv_sem=recv_sem.at[stage, d],
                 device_id=device(db, dx), device_id_type=MESH)))
         return copies
@@ -119,18 +125,13 @@
             chosen = [copy for db, copy in copies if db == sign]
             where_blocks(sign, lambda: [copy.wait_send() for copy in chosen] and None)
 
+    below = (b + blocks - 1) // blocks
+    above = (2 * blocks - 2 - b) // blocks
+    pl.semaphore_wait(barrier, 2 + below + above)
+    stages = [exchange(stage) for stage in range(3)]
+    start(stages[0])
     loads[0].wait()
     loads[1].wait()
-
-    def pack_body(i, carry):
-        pack(q0, 0, i)
-        return carry
-    lax.fori_loop(0, WV, pack_body, 0)
-    below = (b + blocks - 1) // blocks
-    above = (2 * blocks - 2 - b) // blocks
-    pl.semaphore_wait(barrier, slabs - 1 + slabs * (below + above))
-    stages = [exchange(stage) for stage in range(3)]
-    start(stages[0])
     chosen = []
     for w in range(2):
         first = 124 if w == 0 else -4
@@ -143,12 +144,17 @@
         inter[1, x, j] = packet[:, j * 128:(j + 1) * 128]
 
     gathers = []
-    for k, (db, dx) in enumerate(PEERS):
-        gathers.append((db, pltpu.make_async_remote_copy(
-            src_ref=inter.at[1, x], dst_ref=inter.at[1 - db, x],
-            send_sem=isend_sem.at[k], recv_sem=irecv_sem.at[k],
-            device_id=device(db, dx), device_id_type=MESH)))
-    start(gathers)
+    for phase in RELAYS:
+        copies = []
+        for slab, db, dx in phase:
+            k = sum(len(done) for done in gathers) + len(copies)
+            at = lax.rem(x + slab + slabs, slabs)
+            copies.append((db, pltpu.make_async_remote_copy(
+                src_ref=inter.at[1, at], dst_ref=inter.at[1 - db, at],
+                send_sem=isend_sem.at[k], recv_sem=irecv_sem.at[k],
+                device_id=device(db, dx), device_id_type=MESH)))
+        gathers.append(copies)
+    start(gathers[0])
 
     def inner(source, weight):
         def body(i, carry):
@@ -195,7 +201,7 @@
                 target[pl.ds(base + r * 8, 8), :] = (
                     partial[pl.ds(base + r * 8, 8), :] + step * total)
             if stage < 2:
-                pack(target, stage + 1, i)
+                pack(target, stage, i)
             return carry
         lax.fori_loop(0, WV, body, 0)
 
@@ -303,25 +309,28 @@
     w1, w2, w3 = section_weights
     loads[3].wait()
     inner(q0, w1)
+    wait_recv(gathers[0])
+    start(gathers[1])
     wait_recv(stages[0])
     outer(0, field, w1)
     start(stages[1])
 
     inner(field, w2)
-    wait_recv(gathers)
-    interface_step(inter, inter_b, w1)
+    wait_recv(gathers[1])
+    start(gathers[2])
     wait_recv(stages[1])
     outer(1, field, w2)
     start(stages[2])
 
     inner(field, w3)
+    wait_recv(gathers[2])
+    interface_step(inter, inter_b, w1)
     interface_step(inter_b, inter_c, w2)
     for load in (loads[2], loads[4], loads[5]):
         load.wait()
     interface_last(inter_c, w3)
-    wait_send(gathers)
-    for stage in stages[:2]:
-        wait_send(stage)
+    for copies in gathers + stages[:2]:
+        wait_send(copies)
     wait_recv(stages[2])
     outer(2, out_ref, w3)
     wait_send(stages[2])
@@ -350,7 +359,7 @@
         functools.partial(kernel, blocks, slabs),
         out_shape=(pltpu.VMEM((cells, 128), jnp.float32),
                    pltpu.VMEM((2, ROWS, columns), jnp.float32)),
-        in_specs=[any_space] * 6,
+        in_specs=[any_space] * 7,
         out_specs=(vmem, vmem),
         scratch_shapes=[
             pltpu.SMEM((3, 2, NV), jnp.float32),
@@ -361,7 +370,7 @@
             pltpu.VMEM((slabs, NV, 8, 128), jnp.float32),
             pltpu.VMEM((cells, 128), jnp.float32),
             pltpu.VMEM((cells, 128), jnp.float32),
-            pltpu.VMEM((3, 4, WV, 8, 128), jnp.float32),
+            pltpu.VMEM((2, 4, WV, 8, 128), jnp.float32),
             pltpu.VMEM((3, 4, WV, 8, 128), jnp.float32),
             pltpu.VMEM((3, slabs, 3, 8, 128), jnp.float32),
             pltpu.VMEM((3, slabs, 3, 8, 128), jnp.float32),
@@ -369,12 +378,13 @@
             pltpu.SemaphoreType.DMA((6,)),
             pltpu.SemaphoreType.DMA((3, 4)),
             pltpu.SemaphoreType.DMA((3, 4)),
-            pltpu.SemaphoreType.DMA((len(PEERS),)),
-            pltpu.SemaphoreType.DMA((len(PEERS),)),
+            pltpu.SemaphoreType.DMA((sum(len(phase) for phase in RELAYS),)),
+            pltpu.SemaphoreType.DMA((sum(len(phase) for phase in RELAYS),)),
         ],
         compiler_params=pltpu.CompilerParams(collective_id=0, has_side_effects=True),
         name="window",
-    )(jnp.transpose(speeds, (2, 0, 1)), states.reshape(cells, 128), time_steps.reshape(128, 128),
+    )(jnp.transpose(speeds, (2, 0, 1)), states.reshape(WV, ROWS, 8, 128),
+      states.reshape(cells, 128), time_steps.reshape(128, 128),
       jnp.asarray(tables), jnp.transpose(band_src, (2, 0, 1)), jnp.transpose(band_frac, (2, 0, 1)))
     field, arrivals = pl.pallas_call(
         write_out,

time: 26 us -> 27 us (1.038)
  Pallas kernels: 25.2 us -> 26.2 us
    pallas_call x1, Pallas kernels: 24.5 us -> 25.4 us  [shards(): pl.pallas_call(functools.partial(kernel, blocks, slabs), out_shape=(pltpu...]
where the time goes in v4:
time: 27 us; the launch traced here: 26.8 us
  Pallas kernels  26.2 us (97%)
  between operations  0.64 us (2%)
    pallas_call x1, Pallas kernels, shards(): pl.pallas_call(functools.partial(kernel, blocks, slabs), out_shape=(pltpu...  25.4 us
    pallas_call x1, Pallas kernels, shards(): pl.pallas_call(write_out, out_shape=(jax.ShapeDtypeStruct(field.shape, jn...  0.77 us

profile of v4, /device:TPU:32, one launch (start us, length us, event | category | flops | bytes accessed | tf_op | source)
XLA Modules:
  0.0 26.8 jit_solution(12436436211291231338)
XLA Ops:
  0.6 25.4 %window.1 = (f32[640,128]{1,0:T(8,128)S(1)}, f32[2,8,120]{2,1,0:T(8,128)S(1)}) custom-call(f32[3,2,5]{2,1,0:T(2,128)} %bitcast.10, f32[10,8,8,128]{3,2,1,0:T(8,128)} %bitcast.7, f32[640,128]{1,0:T(8,128)} %bitcast.8, f32[128,128]{1,0:T(8,128)} %bitcast.9, f32[4,4,5,8,128]{4,3,2,1,0:T(8,128)} %constant.2.clone.table_hbm, s32[3,2,8]{2,1,0:T(2,128)} %bitcast.11, ...), custom_call_target="tpu_custom_call" | custom-call | tf_op jit(solution)/shard_map/window/pallas_call | solution.py:358
  26.0 0.8 %write_out.1 = (f32[640,128]{1,0:T(8,128)}, f32[2,8,120]{2,1,0:T(8,128)}) custom-call(f32[640,128]{1,0:T(8,128)S(1)} %get-tuple-element.6.field_ref, f32[2,8,120]{2,1,0:T(8,128)S(1)} %get-tuple-element.7.arr_ref), custom_call_target="tpu_custom_call" | custom-call | tf_op jit(solution)/shard_map/write_out/pallas_call | solution.py:389

commit v5 on v4

--- a/solution.py
+++ b/solution.py
@@ -43,7 +43,7 @@
 
 def kernel(blocks, slabs, speeds_hbm, blocks_hbm, states_hbm, steps_hbm, table_hbm, src_hbm, frac_hbm,
            out_ref, arr_ref,
-           speeds, src_ref, frac_ref, q0, dt, table, partial, field, send, halo, inter, inter_b, inter_c,
+           speeds, src_ref, frac_ref, q0, dt, table, partial, field, first, send, halo, inter, inter_b, inter_c,
            load_sem, send_sem, recv_sem, isend_sem, irecv_sem):
     b = lax.axis_index("blk")
     x = lax.axis_index("pitch")
@@ -98,8 +98,7 @@
         send[stage, 2, i] = source[pl.ds(base + 56, 8), :]
         send[stage, 3, i] = source[pl.ds(base, 8), :]
 
-    faces = (blocks_hbm.at[:, :, 7], blocks_hbm.at[:, :, 0],
-             blocks_hbm.at[:, ROWS - 1], blocks_hbm.at[:, 0])
+    faces = (first.at[0], first.at[1], blocks_hbm.at[:, ROWS - 1], blocks_hbm.at[:, 0])
 
     def exchange(stage):
         copies = []
@@ -113,7 +112,8 @@
     def start(copies):
         for sign in (1, -1, 0):
             chosen = [copy for db, copy in copies if db == sign]
-            where_blocks(sign, lambda: [copy.start() for copy in chosen] and None)
+            if chosen:
+                where_blocks(sign, lambda: [copy.start() for copy in chosen] and None)
 
     def wait_recv(copies):
         for sign in (0, 1, -1):
@@ -129,8 +129,12 @@
     above = (2 * blocks - 2 - b) // blocks
     pl.semaphore_wait(barrier, 2 + below + above)
     stages = [exchange(stage) for stage in range(3)]
-    start(stages[0])
+    start([face for face in stages[0] if face[0] != 0])
     loads[0].wait()
+    for i in range(WV):
+        first[0, i] = q0[pl.ds(i * 64 + 7, 8, stride=8), :]
+        first[1, i] = q0[pl.ds(i * 64, 8, stride=8), :]
+    start([face for face in stages[0] if face[0] == 0])
     loads[1].wait()
     chosen = []
     for w in range(2):
@@ -157,10 +161,10 @@
     start(gathers[0])
 
     def inner(source, weight):
-        def body(i, carry):
-            base = pl.multiple_of(i * 64, 64)
-            dbase = pl.multiple_of((i // NV) * 64, 64)
-            a0, a1, a2 = (speeds[k, i // NV, lax.rem(i, NV)] for k in range(3))
+        def update(w, v):
+            base = pl.multiple_of((w * NV + v) * 64, 64)
+            dbase = w * 64
+            a0, a1, a2 = (speeds[k, w, v] for k in range(3))
             centre = -(a0 + a1 + a2) - 6.0 * NU
             axial_low = jnp.where(lane == 0, 0.0, a0 + NU)
             axial_high = jnp.where(lane == 127, 0.0, NU)
@@ -180,14 +184,19 @@
                     total += NU * rows[r + 1]
                 step = weight * dt[pl.ds(dbase + r * 8, 8), :]
                 partial[pl.ds(base + r * 8, 8), :] = q0[pl.ds(base + r * 8, 8), :] + step * total
+
+        def body(v, carry):
+            for w in range(2):
+                update(w, v)
             return carry
-        lax.fori_loop(0, WV, body, 0)
+        lax.fori_loop(0, NV, body, 0)
 
     def outer(stage, target, weight):
-        def body(i, carry):
+        def update(w, v):
+            i = w * NV + v
             base = pl.multiple_of(i * 64, 64)
-            dbase = pl.multiple_of((i // NV) * 64, 64)
-            a1, a2 = (speeds[k, i // NV, lax.rem(i, NV)] for k in range(1, 3))
+            dbase = w * 64
+            a1, a2 = (speeds[k, w, v] for k in range(1, 3))
             pitch_low = jnp.where(sub == 0, a2 + NU, 0.0)
             pitch_high = jnp.where(sub == 7, NU, 0.0)
             for r in range(ROWS):
@@ -200,10 +209,15 @@
                 step = weight * dt[pl.ds(dbase + r * 8, 8), :]
                 target[pl.ds(base + r * 8, 8), :] = (
                     partial[pl.ds(base + r * 8, 8), :] + step * total)
+
+        def body(v, carry):
+            for w in range(2):
+                update(w, v)
             if stage < 2:
-                pack(target, stage, i)
+                for w in range(2):
+                    pack(target, stage, w * NV + v)
             return carry
-        lax.fori_loop(0, WV, body, 0)
+        lax.fori_loop(0, NV, body, 0)
 
     def speed_lanes(k, j):
         def of(w, v):
@@ -370,6 +384,7 @@
             pltpu.VMEM((slabs, NV, 8, 128), jnp.float32),
             pltpu.VMEM((cells, 128), jnp.float32),
             pltpu.VMEM((cells, 128), jnp.float32),
+            pltpu.VMEM((2, WV, 8, 128), jnp.float32),
             pltpu.VMEM((2, 4, WV, 8, 128), jnp.float32),
             pltpu.VMEM((3, 4, WV, 8, 128), jnp.float32),
             pltpu.VMEM((3, slabs, 3, 8, 128), jnp.float32),

time: 27 us -> 26.7 us (0.989)
  Pallas kernels: 26.2 us -> 25.9 us
where the time goes in v5:
time: 26.7 us; the launch traced here: 26.6 us
  Pallas kernels  25.9 us (97%)
  between operations  0.64 us (2%)
    pallas_call x1, Pallas kernels, shards(): pl.pallas_call(functools.partial(kernel, blocks, slabs), out_shape=(pltpu...  25.1 us
    pallas_call x1, Pallas kernels, shards(): pl.pallas_call(write_out, out_shape=(jax.ShapeDtypeStruct(field.shape, jn...  0.77 us

profile of v5, /device:TPU:32, one launch (start us, length us, event | category | flops | bytes accessed | tf_op | source)
XLA Modules:
  0.0 26.6 jit_solution(14648551481862365891)
XLA Ops:
  0.6 25.1 %window.1 = (f32[640,128]{1,0:T(8,128)S(1)}, f32[2,8,120]{2,1,0:T(8,128)S(1)}) custom-call(f32[3,2,5]{2,1,0:T(2,128)} %bitcast.10, f32[10,8,8,128]{3,2,1,0:T(8,128)} %bitcast.7, f32[640,128]{1,0:T(8,128)} %bitcast.8, f32[128,128]{1,0:T(8,128)} %bitcast.9, f32[4,4,5,8,128]{4,3,2,1,0:T(8,128)} %constant.2.clone.table_hbm, s32[3,2,8]{2,1,0:T(2,128)} %bitcast.11, ...), custom_call_target="tpu_custom_call" | custom-call | tf_op jit(solution)/shard_map/window/pallas_call | solution.py:372
  25.8 0.8 %write_out.1 = (f32[640,128]{1,0:T(8,128)}, f32[2,8,120]{2,1,0:T(8,128)}) custom-call(f32[640,128]{1,0:T(8,128)S(1)} %get-tuple-element.6.field_ref, f32[2,8,120]{2,1,0:T(8,128)S(1)} %get-tuple-element.7.arr_ref), custom_call_target="tpu_custom_call" | custom-call | tf_op jit(solution)/shard_map/write_out/pallas_call | solution.py:404

commit v6 on v5

--- a/solution.py
+++ b/solution.py
@@ -91,13 +91,6 @@
             halo[stage, 3] = jnp.zeros((WV, 8, 128), jnp.float32)
         inter[2] = jnp.zeros(inter.shape[1:], jnp.float32)
 
-    def pack(source, stage, i):
-        base = pl.multiple_of(i * 64, 64)
-        send[stage, 0, i] = source[pl.ds(base + 7, 8, stride=8), :]
-        send[stage, 1, i] = source[pl.ds(base, 8, stride=8), :]
-        send[stage, 2, i] = source[pl.ds(base + 56, 8), :]
-        send[stage, 3, i] = source[pl.ds(base, 8), :]
-
     faces = (first.at[0], first.at[1], blocks_hbm.at[:, ROWS - 1], blocks_hbm.at[:, 0])
 
     def exchange(stage):
@@ -118,7 +111,8 @@
     def wait_recv(copies):
         for sign in (0, 1, -1):
             chosen = [copy for db, copy in copies if db == sign]
-            where_blocks(-sign, lambda: [copy.wait_recv() for copy in chosen] and None)
+            if chosen:
+                where_blocks(-sign, lambda: [copy.wait_recv() for copy in chosen] and None)
 
     def wait_send(copies):
         for sign in (0, 1, -1):
@@ -191,21 +185,17 @@
             return carry
         lax.fori_loop(0, NV, body, 0)
 
-    def outer(stage, target, weight):
+    def outer_pitch(stage, target, weight):
         def update(w, v):
             i = w * NV + v
             base = pl.multiple_of(i * 64, 64)
             dbase = w * 64
-            a1, a2 = (speeds[k, w, v] for k in range(1, 3))
+            a2 = speeds[2, w, v]
             pitch_low = jnp.where(sub == 0, a2 + NU, 0.0)
             pitch_high = jnp.where(sub == 7, NU, 0.0)
             for r in range(ROWS):
                 total = pitch_low * halo[stage, 0, i, pl.ds(r, 1), :]
                 total += pitch_high * halo[stage, 1, i, pl.ds(r, 1), :]
-                if r == 0:
-                    total += (a1 + NU) * halo[stage, 2, i]
-                if r == ROWS - 1:
-                    total += NU * halo[stage, 3, i]
                 step = weight * dt[pl.ds(dbase + r * 8, 8), :]
                 target[pl.ds(base + r * 8, 8), :] = (
                     partial[pl.ds(base + r * 8, 8), :] + step * total)
@@ -213,11 +203,49 @@
         def body(v, carry):
             for w in range(2):
                 update(w, v)
-            if stage < 2:
-                for w in range(2):
-                    pack(target, stage, w * NV + v)
             return carry
         lax.fori_loop(0, NV, body, 0)
+
+    def outer_radial(stage, target, weight):
+        def body(v, carry):
+            for w in range(2):
+                i = w * NV + v
+                a1 = speeds[1, w, v]
+                for r, side, factor in ((ROWS - 1, 3, NU), (0, 2, a1 + NU)):
+                    place = pl.ds(pl.multiple_of(i * 64, 64) + r * 8, 8)
+                    step = weight * dt[w * 64 + r * 8:w * 64 + r * 8 + 8, :]
+                    value = target[place, :] + (step * factor) * halo[stage, side, i]
+                    target[place, :] = value
+                    if stage < 2:
+                        send[stage, 2 if r else 3, i] = value
+            return carry
+        lax.fori_loop(0, NV, body, 0)
+
+    def pack_pitch(stage, source):
+        def body(v, carry):
+            for w in range(2):
+                i = w * NV + v
+                base = pl.multiple_of(i * 64, 64)
+                send[stage, 0, i] = source[pl.ds(base + 7, 8, stride=8), :]
+                send[stage, 1, i] = source[pl.ds(base, 8, stride=8), :]
+            return carry
+        lax.fori_loop(0, NV, body, 0)
+
+    def pitch_of(copies):
+        return [copy for copy in copies if copy[0] == 0]
+
+    def radial_of(copies):
+        return [copy for copy in copies if copy[0] != 0]
+
+    def arrive(stage, target, weight):
+        wait_recv(pitch_of(stages[stage]))
+        outer_pitch(stage, target, weight)
+        wait_recv(radial_of(stages[stage]))
+        outer_radial(stage, target, weight)
+        if stage < 2:
+            start(radial_of(stages[stage + 1]))
+            pack_pitch(stage, target)
+            start(pitch_of(stages[stage + 1]))
 
     def speed_lanes(k, j):
         def of(w, v):
@@ -325,16 +353,12 @@
     inner(q0, w1)
     wait_recv(gathers[0])
     start(gathers[1])
-    wait_recv(stages[0])
-    outer(0, field, w1)
-    start(stages[1])
+    arrive(0, field, w1)
 
     inner(field, w2)
     wait_recv(gathers[1])
     start(gathers[2])
-    wait_recv(stages[1])
-    outer(1, field, w2)
-    start(stages[2])
+    arrive(1, field, w2)
 
     inner(field, w3)
     wait_recv(gathers[2])
@@ -345,8 +369,7 @@
     interface_last(inter_c, w3)
     for copies in gathers + stages[:2]:
         wait_send(copies)
-    wait_recv(stages[2])
-    outer(2, out_ref, w3)
+    arrive(2, out_ref, w3)
     wait_send(stages[2])
 
 

time: 26.7 us -> 26.7 us (level)
  no operation moved by 1% of the time
where the time goes in v6:
time: 26.7 us; the launch traced here: 26.6 us
  Pallas kernels  26 us (97%)
  between operations  0.64 us (2%)
    pallas_call x1, Pallas kernels, shards(): pl.pallas_call(functools.partial(kernel, blocks, slabs), out_shape=(pltpu...  25.2 us
    pallas_call x1, Pallas kernels, shards(): pl.pallas_call(write_out, out_shape=(jax.ShapeDtypeStruct(field.shape, jn...  0.77 us

profile of v6, /device:TPU:32, one launch (start us, length us, event | category | flops | bytes accessed | tf_op | source)
XLA Modules:
  0.0 26.6 jit_solution(14941625830602777096)
XLA Ops:
  0.6 25.2 %window.1 = (f32[640,128]{1,0:T(8,128)S(1)}, f32[2,8,120]{2,1,0:T(8,128)S(1)}) custom-call(f32[3,2,5]{2,1,0:T(2,128)} %bitcast.10, f32[10,8,8,128]{3,2,1,0:T(8,128)} %bitcast.7, f32[640,128]{1,0:T(8,128)} %bitcast.8, f32[128,128]{1,0:T(8,128)} %bitcast.9, f32[4,4,5,8,128]{4,3,2,1,0:T(8,128)} %constant.2.clone.table_hbm, s32[3,2,8]{2,1,0:T(2,128)} %bitcast.11, ...), custom_call_target="tpu_custom_call" | custom-call | tf_op jit(solution)/shard_map/window/pallas_call | solution.py:395
  25.8 0.8 %write_out.1 = (f32[640,128]{1,0:T(8,128)}, f32[2,8,120]{2,1,0:T(8,128)}) custom-call(f32[640,128]{1,0:T(8,128)S(1)} %get-tuple-element.6.field_ref, f32[2,8,120]{2,1,0:T(8,128)S(1)} %get-tuple-element.7.arr_ref), custom_call_target="tpu_custom_call" | custom-call | tf_op jit(solution)/shard_map/write_out/pallas_call | solution.py:427
